TPU v7x, 256 devices: a whole 4x4x8 slice. The times are simulated.
256 devices in a mesh: dp: 4 (over y_lo, core), tm: 4 (over x), rows: 16 (over z, y_hi).
Axes of the slice: x: 4, y: 4 (y_hi: 2, y_lo: 2; y = y_hi * 2 + y_lo), z: 8, core: 2. Of those that a mesh axis runs over, the one named last changes fastest.
Arguments:
- latents: bfloat16 [4, 8, 16, 30, 512], P('dp', 'tm', 'rows'), may hold values from -6 to 6
- grad_out: bfloat16 [4, 8, 32, 60, 256], P('dp', 'tm', 'rows'), may hold values from -6 to 6
- kernel: bfloat16 [3, 3, 3, 512, 256], replicated, may hold values from -0.0546875 to 0.0546875
Outputs:
- grad_latents: bfloat16 [4, 8, 16, 30, 512], P('dp', 'tm', 'rows')
- weight_grad: float32 [512, 3, 3, 3, 256], P(('dp', 'tm', 'rows'))
All inputs are finite; a program needn't handle non-finite values.
Results may differ from a plain program's by a relative error of at most 0.001.
Values may be sent and summed in bfloat16 or wider, within the bound.
A program may use at most 128 MiB of HBM per device.

v0:
```python
import jax
import jax.numpy as jnp
from jax import lax
from jax.sharding import PartitionSpec as P


def shift_from(shard, axis, by):
    peers = lax.axis_size(axis)
    pairs = [(i, i + by) for i in range(peers) if 0 <= i + by < peers]
    return lax.ppermute(shard, axis, pairs)


def pool_pairs(values, dim):
    n = values.shape[dim] // 2
    pad = [(0, 0)] * values.ndim
    pad[dim] = (1, 1)
    ext = jnp.pad(values, pad)
    out = []
    for i in range(3):
        start = 2 - i
        a = lax.slice_in_dim(ext, start, start + 2 * n - 1, stride=2, axis=dim)
        b = lax.slice_in_dim(ext, start + 1, start + 2 * n, stride=2, axis=dim)
        out.append(a + b)
    return jnp.stack(out, axis=dim + 1)


def body(latents, grad_out, kernel):
    frames = grad_out.shape[1]
    height = grad_out.shape[2]
    width = grad_out.shape[3]
    channels = latents.shape[4]
    outputs = grad_out.shape[4]
    devices = lax.axis_size("dp") * lax.axis_size("tm") * lax.axis_size("rows")
    factor = float(devices * frames * height * width) ** (-0.5)
    slab_count = lax.axis_size("rows")
    slab = lax.axis_index("rows")
    grad_whole = lax.all_gather(grad_out[0], "rows", axis=1, tiled=True)
    whole_height = grad_whole.shape[1]
    padded_rows = jnp.pad(grad_whole, ((0, 0), (1, 1), (0, 0), (0, 0)))
    near = lax.dynamic_slice_in_dim(padded_rows, slab * height, height + 2, axis=1)
    later = shift_from(near, "tm", -1)
    grad_all = jnp.concatenate([near, later], axis=0)
    grad_all = jnp.pad(grad_all, ((0, 0), (0, 0), (1, 1), (0, 0)))
    patches = []
    for a in range(3):
        for i in range(3):
            for j in range(3):
                patches.append(
                    grad_all[2 - a : 2 - a + frames, 2 - i : 2 - i + height, 2 - j : 2 - j + width]
                )
    patches = jnp.stack(patches, axis=3).reshape(frames * height * width, 27, outputs)
    grad_up = lax.dot_general(
        patches,
        kernel.reshape(27, channels, outputs),
        (((1, 2), (0, 2)), ((), ())),
        preferred_element_type=jnp.float32,
    )
    pooled = grad_up.reshape(frames, height // 2, 2, width // 2, 2, channels).sum(axis=(2, 4))
    grad_latents = pooled.astype(jnp.bfloat16)[None]
    groups = lax.axis_size("dp") * lax.axis_size("tm")
    share = channels // devices
    earlier = shift_from(latents, "tm", 1)
    with_earlier = jnp.concatenate([earlier, latents], axis=1)
    lead = with_earlier.shape[:4]
    regrouped = with_earlier.reshape(lead + (groups, slab_count, share))
    regrouped = jnp.swapaxes(regrouped, 4, 5).reshape(lead + (channels,))
    owned = lax.all_to_all(regrouped, "rows", split_axis=4, concat_axis=2, tiled=True)[0]
    group_channels = owned.shape[3]
    taps_a = jnp.stack([owned[a : a + frames] for a in range(3)], axis=0)
    pooled_grad = pool_pairs(pool_pairs(grad_whole.astype(jnp.float32), 1), 3)
    scaled = pooled_grad * 65537.0
    top = scaled - (scaled - pooled_grad)
    both = jnp.stack([top, pooled_grad - top], axis=0).astype(jnp.bfloat16)
    term = jnp.einsum("afrsc,xfrisjo->caijxo", taps_a, both, preferred_element_type=jnp.float32)
    term = (term[..., 0, :] + term[..., 1, :]) * factor
    term = term.reshape(group_channels, 3, 3, 3, outputs)
    term = lax.psum_scatter(term, "dp", scatter_dimension=0, tiled=True)
    weight_grad = lax.psum_scatter(term, "tm", scatter_dimension=0, tiled=True)
    return (grad_latents, weight_grad)


def solution(mesh):
    in_specs = (P("dp", "tm", "rows", None, None), P("dp", "tm", "rows", None, None), P())
    out_specs = (P("dp", "tm", "rows", None, None), P(("dp", "tm", "rows"), None, None, None, None))
    return jax.shard_map(body, mesh=mesh, in_specs=in_specs, out_specs=out_specs, check_vma=False)
```

profile of v0, /device:TPU:8, one launch (start us, length us, event | category | flops | bytes accessed | tf_op | source)
XLA Modules:
  0.0 254.9 jit_solution(13434810595302571663)
XLA Ops:
  7.2 1.6 copy.131
  8.8 3.4 %collective-permute-start.1 = (bf16[1,2,1,30,512]{4,1,3,2,0:T(2,128)(2,1)}, bf16[1,2,1,30,512]{4,1,3,2,0:T(2,128)(2,1)S(1)}, u32[]{:S(2)}, u32[]{:S(2)}) collective-permute-start(bf16[1,2,1,30,512]{4,1,3,2,0:T(2,128)(2,1)} %param.3), channel_id=1, source_target_pairs={{0,16},{16,32},{32,48},{1,17},{17,33},{33,49},{2,18},{18,34},{34,5... | collective-permute-start | bytes 184328 | tf_op jit(solution)/shard_map/ppermute | solution.py:10
  12.2 2.2 collective-permute-done.1
  14.4 1.0 pad_maximum_fusion.2
  16.5 1.6 reshape.331
  18.1 10.3 %all-to-all-start = ((bf16[16,2,1920]{2,1,0:T(2,128)(2,1)}), bf16[16,2,1920]{2,1,0:T(2,128)(2,1)S(1)}, u32[]{:S(2)}, u32[]{:S(2)}) async-start(bf16[16,2,1920]{2,1,0:T(2,128)(2,1)} %reshape.331), calls=%async_computation | async-start | bytes 245760 | tf_op jit(solution)/shard_map/all_to_all | solution.py:67
  29.7 10.4 %all-to-all-done = bf16[16,2,1920]{2,1,0:T(2,128)(2,1)S(1)} async-done(((bf16[16,2,1920]{2,1,0:T(2,128)(2,1)}), bf16[16,2,1920]{2,1,0:T(2,128)(2,1)S(1)}, u32[]{:S(2)}, u32[]{:S(2)}) %all-to-all-start) | async-done | bytes 122912 | tf_op jit(solution)/shard_map/all_to_all | solution.py:67
  40.1 1.4 reshape.332
  41.7 56.5 %all-gather.3.cloned.1.call-done = bf16[1,2,32,60,256]{4,3,2,1,0:T(8,128)(2,1)} async-done(((bf16[1,2,2,60,256]{4,3,2,1,0:T(8,128)(2,1)}), bf16[1,2,32,60,256]{4,3,2,1,0:T(8,128)(2,1)}) %all-gather.3.cloned.1.call-update) | async-done | bytes 1966096 | tf_op jit(solution)/shard_map/all_gather | solution.py:37
  98.2 1.1 pad_dynamic-slice_fusion.3
  100.4 1.0 add_bitcast_fusion.5
  101.5 3.3 %select_maximum_fusion = f32[2,16,3,62,256]{4,3,1,0,2:T(8,128)} fusion(f32[2,16,1,60,256]{4,3,1,0,2:T(8,128)S(1)} %get-tuple-element.14, f32[2,16,1,60,256]{4,3,1,0,2:T(8,128)S(1)} %get-tuple-element.13, f32[2,16,1,60,256]{4,3,1,0,2:T(8,128)S(1)} %get-tuple-element.12), kind=kLoop, calls=%fused_computation.11 | loop fusion | flops 12189696 | bytes 11993088 | tf_op jit(solution)/shard_map/stack | solution.py:24
  104.8 14.3 %slice.173 = f32[2,16,3,30,256]{4,3,1,0,2:T(8,128)} slice(f32[2,16,3,62,256]{4,3,1,0,2:T(8,128)} %select_maximum_fusion), slice={[0:2:1], [0:16:1], [0:3:1], [2:61:2], [0:256:1]} | slice | bytes 5898240 | tf_op jit(solution)/shard_map/slice | solution.py:21
  119.1 14.3 %slice.174 = f32[2,16,3,30,256]{4,3,1,0,2:T(8,128)} slice(f32[2,16,3,62,256]{4,3,1,0,2:T(8,128)} %select_maximum_fusion), slice={[0:2:1], [0:16:1], [0:3:1], [3:62:2], [0:256:1]} | slice | bytes 5898240 | tf_op jit(solution)/shard_map/slice | solution.py:22
  133.4 14.2 %slice.175 = f32[2,16,3,30,256]{4,3,1,0,2:T(8,128)} slice(f32[2,16,3,62,256]{4,3,1,0,2:T(8,128)} %select_maximum_fusion), slice={[0:2:1], [0:16:1], [0:3:1], [1:60:2], [0:256:1]} | slice | bytes 5898240 | tf_op jit(solution)/shard_map/slice | solution.py:21
  147.6 14.2 %slice.176 = f32[2,16,3,30,256]{4,3,1,0,2:T(8,128)} slice(f32[2,16,3,62,256]{4,3,1,0,2:T(8,128)} %select_maximum_fusion), slice={[0:2:1], [0:16:1], [0:3:1], [0:59:2], [0:256:1]} | slice | bytes 5898240 | tf_op jit(solution)/shard_map/slice | solution.py:21
  161.7 1.3 collective-permute-start
  163.6 7.2 %add_bitcast_fusion.2 = (f32[1,2,16,3,30,1,256]{6,4,2,1,5,3,0:T(8,128)S(1)}, f32[1,2,16,3,30,1,256]{6,4,2,1,5,3,0:T(8,128)S(1)}, f32[1,2,16,3,30,1,256]{6,4,2,1,5,3,0:T(8,128)S(1)}) fusion(f32[2,16,3,30,256]{4,3,1,0,2:T(8,128)} %slice.173, f32[2,16,3,30,256]{4,3,1,0,2:T(8,128)} %slice.174, f32[2,16,3,30,256]{4,3,1,0,2:T(8,128)} %slice.175, ...), kind=kLoop, calls=%fused_computation.18 | loop fusion | flops 2211840 | bytes 20643840 | tf_op jit(solution)/shard_map/stack | solution.py:24
  170.8 2.2 fusion.1
  173.0 1.7 fusion.9
  174.8 1.1 fusion.17
  176.8 0.7 copy_dynamic-update-slice_fusion.26
  180.7 0.7 copy_dynamic-update-slice_fusion.25
  181.3 0.7 copy_dynamic-update-slice_fusion.24
  182.0 0.7 copy_dynamic-update-slice_fusion.23
  182.7 0.7 copy_dynamic-update-slice_fusion.22
  183.4 0.7 copy_dynamic-update-slice_fusion.21
  184.1 0.7 copy_dynamic-update-slice_fusion.20
  185.4 0.7 copy_dynamic-update-slice_fusion.18
  186.1 0.7 copy_dynamic-update-slice_fusion.17
  186.7 0.7 copy_dynamic-update-slice_fusion.16
  187.4 0.7 copy_dynamic-update-slice_fusion.15
  189.4 0.7 copy_dynamic-update-slice_fusion.12
  190.1 0.7 copy_dynamic-update-slice_fusion.11
  190.8 0.7 copy_dynamic-update-slice_fusion.10
  191.4 0.7 copy_dynamic-update-slice_fusion.9
  192.1 0.7 copy_dynamic-update-slice_fusion.8
  192.8 0.7 copy_dynamic-update-slice_fusion.7
  193.5 0.7 copy_dynamic-update-slice_fusion.6
  194.2 0.7 copy_dynamic-update-slice_fusion.5
  194.9 0.7 copy_dynamic-update-slice_fusion.4
  196.2 0.7 copy_dynamic-update-slice_fusion.2
  196.9 0.7 copy_dynamic-update-slice_fusion.1
  197.5 0.7 copy_dynamic-update-slice_fusion
  198.2 6.1 %fusion.13 = bf16[2,30,512]{2,1,0:T(8,128)(2,1)S(1)} fusion(bf16[27,512,256,1,1,1]{2,1,0,5,4,3:T(8,128)(2,1)} %bitcast.141, bf16[2,1,2,30,2,27,256]{6,3,5,4,2,0,1:T(8,128)(2,1)} %copy_dynamic-update-slice_fusion), kind=kOutput, calls=%fused_computation.29 | convolution fusion | flops 1698785280 | bytes 10457088 | tf_op jit(solution)/shard_map/dot_general | solution.py:52
  204.4 0.7 copy.192
  205.1 41.7 %all-reduce.7.cloned.1.call-done = f32[8,3,3,3,256]{4,0,1,3,2:T(8,128)} async-done(((f32[8,3,3,3,256]{4,0,1,3,2:T(8,128)}), f32[8,3,3,3,256]{4,0,1,3,2:T(8,128)}) %all-reduce.7.cloned.1.call-update) | async-done | bytes 221200
  246.8 1.0 constant_dynamic-slice_fusion
  (56 shorter events, 10.8 us)
Async XLA Ops:
  7.2 21.3 %copy-start.1 = (u32[256]{0:T(256)S(1)}, u32[256]{0:T(256)}, u32[]{:S(2)}) copy-start(u32[256]{0:T(256)} %constant.32) | copy-start | bytes 3076
  7.2 91.0 %all-gather.3.cloned.1.call-start = ((), (), s32[]{:S(2)}) async-start(), calls=%async_computation.3 | async-start | bytes 2228224 | tf_op jit(solution)/shard_map/all_gather | solution.py:37
  8.8 5.6 %collective-permute-start.1 = (bf16[1,2,1,30,512]{4,1,3,2,0:T(2,128)(2,1)}, bf16[1,2,1,30,512]{4,1,3,2,0:T(2,128)(2,1)S(1)}, u32[]{:S(2)}, u32[]{:S(2)}) collective-permute-start(bf16[1,2,1,30,512]{4,1,3,2,0:T(2,128)(2,1)} %param.3), channel_id=1, source_target_pairs={{0,16},{16,32},{32,48},{1,17},{17,33},{33,49},{2,18},{18,34},{34,5... | collective-permute-start | bytes 184328 | tf_op jit(solution)/shard_map/ppermute | solution.py:10
  18.1 22.0 %all-to-all-start = ((bf16[16,2,1920]{2,1,0:T(2,128)(2,1)}), bf16[16,2,1920]{2,1,0:T(2,128)(2,1)S(1)}, u32[]{:S(2)}, u32[]{:S(2)}) async-start(bf16[16,2,1920]{2,1,0:T(2,128)(2,1)} %reshape.331), calls=%async_computation | async-start | bytes 245760 | tf_op jit(solution)/shard_map/all_to_all | solution.py:67
  28.4 169.8 %reduce-scatter.3.cloned.1.call-start = ((), (), s32[]{:S(2)}) async-start(), calls=%async_computation.2 | async-start | bytes 1105920 | tf_op jit(solution)/shard_map/reduce_scatter | solution.py:77
  98.2 1.7 copy-start
  161.7 14.3 %collective-permute-start = (bf16[2,4,60,256]{3,2,1,0:T(8,128)(2,1)S(1)}, bf16[2,4,60,256]{3,2,1,0:T(8,128)(2,1)S(1)}, u32[]{:S(2)}, u32[]{:S(2)}) collective-permute-start(bf16[2,4,60,256]{3,2,1,0:T(8,128)(2,1)S(1)} %pad_dynamic-slice_fusion.3), channel_id=1, source_target_pairs={{16,0},{32,16},{48,32},{17,1},{33,17},{49,33},{18,2},{34,18},{50,3... | collective-permute-start | bytes 737288 | tf_op jit(solution)/shard_map/ppermute | solution.py:10
  175.9 70.9 %all-reduce.7.cloned.1.call-start = ((), (), s32[]{:S(2)}) async-start(), calls=%async_computation.4 | async-start | bytes 442368
Sparse Core Ops, SparseCore 0:
  10.6 87.5 all-gather.2
  176.0 19.1 reduce-scatter.2
  198.4 48.3 all-reduce.6
where the time goes:
time: 257 us; the launch traced here: 255 us
  waiting for transfers between devices  111 us (43%)
  local copies, waits for them, and re-layouts  89.7 us (35%)
  other arithmetic  16.5 us (6%)
  starting transfers between devices  15.3 us (6%)
  between operations  14.8 us (6%)
  matrix products  7.84 us (3%)
    all_gather x1, waiting for transfers between devices, body(): grad_whole = lax.all_gather(grad_out[0], 'rows', axis=1, tiled=True)  56.5 us
    slice x3, local copies, waits for them, and re-layouts, pool_pairs(): a = lax.slice_in_dim(ext, start, start + 2 * n - 1, stride=2, axis=dim)  42.7 us
    unnamed x4, waiting for transfers between devices  41.8 us
    unnamed x37, local copies, waits for them, and re-layouts  25.6 us
    slice x1, local copies, waits for them, and re-layouts, pool_pairs(): b = lax.slice_in_dim(ext, start + 1, start + 2 * n, stride=2, axis=dim)  14.3 us
    another operation x3, other arithmetic, pool_pairs(): return jnp.stack(out, axis=dim + 1)  11.5 us
    all_to_all x1, waiting for transfers between devices, body(): lax.all_to_all(regrouped, 'rows', split_axis=4, concat_axis=2, tiled=True)  10.4 us
    all_to_all x1, starting transfers between devices, body(): lax.all_to_all(regrouped, 'rows', split_axis=4, concat_axis=2, tiled=True)  10.3 us
  transfers between devices with their start and end apart: 6, of which 4 were waited for; matrix products, arithmetic and copies ran while one was open for 19% of the time, Pallas kernels for 0%

commit v1 on v0

--- a/solution.py
+++ b/solution.py
@@ -34,7 +34,9 @@
     factor = float(devices * frames * height * width) ** (-0.5)
     slab_count = lax.axis_size("rows")
     slab = lax.axis_index("rows")
-    grad_whole = lax.all_gather(grad_out[0], "rows", axis=1, tiled=True)
+    grad_whole = jnp.concatenate(
+        lax.all_to_all(jnp.stack([grad_out[0]] * lax.axis_size("rows")), "rows", 0, 0), axis=1
+    )
     whole_height = grad_whole.shape[1]
     padded_rows = jnp.pad(grad_whole, ((0, 0), (1, 1), (0, 0), (0, 0)))
     near = lax.dynamic_slice_in_dim(padded_rows, slab * height, height + 2, axis=1)

time: 257 us -> 250 us (0.973)
  waiting for transfers between devices: 111 us -> 87.3 us
  blocking collectives: 0 us -> 21.2 us
  starting transfers between devices: 15.3 us -> 8.79 us
    all_gather x1 -> x0, waiting for transfers between devices: 56.5 us -> none  [body(): grad_whole = lax.all_gather(grad_out[0], 'rows', axis=1, tiled=True)]
    all_to_all x1, waiting for transfers between devices: 10.4 us -> 44.5 us  [body(): lax.all_to_all(jnp.stack([grad_out[0]] * lax.axis_size('rows')), 'rows',...]
    all_to_all x0 -> x1, blocking collectives: none -> 21.2 us  [body(): lax.all_to_all(regrouped, 'rows', split_axis=4, concat_axis=2, tiled=True)]
    all_to_all x1, starting transfers between devices: 10.3 us -> 3.72 us  [body(): lax.all_to_all(jnp.stack([grad_out[0]] * lax.axis_size('rows')), 'rows',...]
    unnamed x37 -> x38, local copies, waits for them, and re-layouts: 25.6 us -> 24 us
    unnamed x4 -> x3, waiting for transfers between devices: 41.8 us -> 40.6 us
  transfers between devices with their start and end apart: 6 -> 5, of which waited for: 4 -> 3; matrix products, arithmetic and copies ran while one was open for 19% -> 18% of each run, Pallas kernels for 0% -> 0%
where the time goes in v1:
time: 250 us; the launch traced here: 248 us
  local copies, waits for them, and re-layouts  91.3 us (37%)
  waiting for transfers between devices  87.3 us (35%)
  blocking collectives  21.2 us (8%)
  other arithmetic  16.5 us (7%)
  between operations  15.1 us (6%)
  starting transfers between devices  8.79 us (4%)
  matrix products  7.84 us (3%)
    all_to_all x1, waiting for transfers between devices, body(): lax.all_to_all(jnp.stack([grad_out[0]] * lax.axis_size('rows')), 'rows',...  44.5 us
    slice x3, local copies, waits for them, and re-layouts, pool_pairs(): a = lax.slice_in_dim(ext, start, start + 2 * n - 1, stride=2, axis=dim)  42.7 us
    unnamed x3, waiting for transfers between devices  40.6 us
    unnamed x38, local copies, waits for them, and re-layouts  24 us
    all_to_all x1, blocking collectives, body(): lax.all_to_all(regrouped, 'rows', split_axis=4, concat_axis=2, tiled=True)  21.2 us
    slice x1, local copies, waits for them, and re-layouts, pool_pairs(): b = lax.slice_in_dim(ext, start + 1, start + 2 * n, stride=2, axis=dim)  14.3 us
    another operation x3, other arithmetic, pool_pairs(): return jnp.stack(out, axis=dim + 1)  11.5 us
    dot_general x1, matrix products, body(): lax.dot_general(patches, kernel.reshape(27, channels, outputs), (((1, 2),...  6.12 us
  transfers between devices with their start and end apart: 5, of which 3 were waited for; matrix products, arithmetic and copies ran while one was open for 18% of the time, Pallas kernels for 0%

profile of v1, /device:TPU:8, one launch (start us, length us, event | category | flops | bytes accessed | tf_op | source)
XLA Modules:
  0.0 248.0 jit_solution(839780133481830368)
XLA Ops:
  7.2 3.5 %collective-permute-start.1 = (bf16[1,2,1,30,512]{4,1,3,2,0:T(2,128)(2,1)}, bf16[1,2,1,30,512]{4,1,3,2,0:T(2,128)(2,1)S(1)}, u32[]{:S(2)}, u32[]{:S(2)}) collective-permute-start(bf16[1,2,1,30,512]{4,1,3,2,0:T(2,128)(2,1)} %param.3), channel_id=1, source_target_pairs={{0,16},{16,32},{32,48},{1,17},{17,33},{33,49},{2,18},{18,34},{34,5... | collective-permute-start | bytes 184328 | tf_op jit(solution)/shard_map/ppermute | solution.py:10
  10.7 2.2 collective-permute-done.1
  12.9 1.0 pad_maximum_fusion.2
  15.0 1.0 reshape.339
  15.9 21.2 %all_to_all.20 = bf16[16,2,1920]{2,1,0:T(2,128)(2,1)S(1)} all-to-all(bf16[16,2,1920]{2,1,0:T(2,128)(2,1)S(1)} %reshape.339), channel_id=1, replica_groups=mesh['dp'=4,'tm'=4,'rows'=16] {'rows'}, dimensions={0} | all-to-all | bytes 245760 | tf_op jit(solution)/shard_map/all_to_all | solution.py:69
  37.1 2.3 stack.129
  39.4 3.7 %all-to-all-start = ((bf16[16,2,2,60,256]{4,2,3,1,0:T(2,128)(2,1)}), bf16[16,2,2,60,256]{4,2,3,1,0:T(2,128)(2,1)S(1)}, u32[]{:S(2)}, u32[]{:S(2)}) async-start(bf16[16,2,2,60,256]{4,2,3,1,0:T(2,128)(2,1)} %stack.129), calls=%async_computation | async-start | bytes 3932160 | tf_op jit(solution)/shard_map/all_to_all | solution.py:38
  44.4 1.4 reshape.340
  46.0 44.5 %all-to-all-done = bf16[16,2,2,60,256]{4,2,3,1,0:T(2,128)(2,1)S(1)} async-done(((bf16[16,2,2,60,256]{4,2,3,1,0:T(2,128)(2,1)}), bf16[16,2,2,60,256]{4,2,3,1,0:T(2,128)(2,1)S(1)}, u32[]{:S(2)}, u32[]{:S(2)}) %all-to-all-start) | async-done | bytes 1966112 | tf_op jit(solution)/shard_map/all_to_all | solution.py:38
  90.5 1.3 copy-done
  91.8 1.9 copy.131
  94.4 1.0 add_bitcast_fusion.5
  95.4 3.3 %select_maximum_fusion = f32[2,16,3,62,256]{4,3,1,0,2:T(8,128)} fusion(f32[2,16,1,60,256]{4,3,1,0,2:T(8,128)S(1)} %get-tuple-element.14, f32[2,16,1,60,256]{4,3,1,0,2:T(8,128)S(1)} %get-tuple-element.13, f32[2,16,1,60,256]{4,3,1,0,2:T(8,128)S(1)} %get-tuple-element.12), kind=kLoop, calls=%fused_computation.11 | loop fusion | flops 12189696 | bytes 11993088 | tf_op jit(solution)/shard_map/stack | solution.py:24
  98.7 14.3 %slice.173 = f32[2,16,3,30,256]{4,3,1,0,2:T(8,128)} slice(f32[2,16,3,62,256]{4,3,1,0,2:T(8,128)} %select_maximum_fusion), slice={[0:2:1], [0:16:1], [0:3:1], [2:61:2], [0:256:1]} | slice | bytes 5898240 | tf_op jit(solution)/shard_map/slice | solution.py:21
  113.0 14.3 %slice.174 = f32[2,16,3,30,256]{4,3,1,0,2:T(8,128)} slice(f32[2,16,3,62,256]{4,3,1,0,2:T(8,128)} %select_maximum_fusion), slice={[0:2:1], [0:16:1], [0:3:1], [3:62:2], [0:256:1]} | slice | bytes 5898240 | tf_op jit(solution)/shard_map/slice | solution.py:22
  127.3 14.2 %slice.175 = f32[2,16,3,30,256]{4,3,1,0,2:T(8,128)} slice(f32[2,16,3,62,256]{4,3,1,0,2:T(8,128)} %select_maximum_fusion), slice={[0:2:1], [0:16:1], [0:3:1], [1:60:2], [0:256:1]} | slice | bytes 5898240 | tf_op jit(solution)/shard_map/slice | solution.py:21
  141.4 14.2 %slice.176 = f32[2,16,3,30,256]{4,3,1,0,2:T(8,128)} slice(f32[2,16,3,62,256]{4,3,1,0,2:T(8,128)} %select_maximum_fusion), slice={[0:2:1], [0:16:1], [0:3:1], [0:59:2], [0:256:1]} | slice | bytes 5898240 | tf_op jit(solution)/shard_map/slice | solution.py:21
  155.6 1.3 collective-permute-start
  157.4 7.2 %add_bitcast_fusion.2 = (f32[1,2,16,3,30,1,256]{6,4,2,1,5,3,0:T(8,128)S(1)}, f32[1,2,16,3,30,1,256]{6,4,2,1,5,3,0:T(8,128)S(1)}, f32[1,2,16,3,30,1,256]{6,4,2,1,5,3,0:T(8,128)S(1)}) fusion(f32[2,16,3,30,256]{4,3,1,0,2:T(8,128)} %slice.173, f32[2,16,3,30,256]{4,3,1,0,2:T(8,128)} %slice.174, f32[2,16,3,30,256]{4,3,1,0,2:T(8,128)} %slice.175, ...), kind=kLoop, calls=%fused_computation.18 | loop fusion | flops 2211840 | bytes 20643840 | tf_op jit(solution)/shard_map/stack | solution.py:24
  164.7 2.2 fusion.1
  166.9 1.7 fusion.9
  168.6 1.1 fusion.17
  170.7 0.7 copy_dynamic-update-slice_fusion.26
  174.6 0.7 copy_dynamic-update-slice_fusion.25
  175.2 0.7 copy_dynamic-update-slice_fusion.24
  175.9 0.7 copy_dynamic-update-slice_fusion.23
  176.6 0.7 copy_dynamic-update-slice_fusion.22
  177.3 0.7 copy_dynamic-update-slice_fusion.21
  178.0 0.7 copy_dynamic-update-slice_fusion.20
  178.6 0.7 copy_dynamic-update-slice_fusion.19
  179.3 0.7 copy_dynamic-update-slice_fusion.18
  180.7 0.7 copy_dynamic-update-slice_fusion.16
  181.3 0.7 copy_dynamic-update-slice_fusion.15
  182.0 0.7 copy_dynamic-update-slice_fusion.14
  182.7 0.7 copy_dynamic-update-slice_fusion.13
  184.7 0.7 copy_dynamic-update-slice_fusion.10
  185.4 0.7 copy_dynamic-update-slice_fusion.9
  186.0 0.7 copy_dynamic-update-slice_fusion.8
  186.7 0.7 copy_dynamic-update-slice_fusion.7
  187.4 0.7 copy_dynamic-update-slice_fusion.6
  188.1 0.7 copy_dynamic-update-slice_fusion.5
  188.7 0.7 copy_dynamic-update-slice_fusion.4
  189.4 0.7 copy_dynamic-update-slice_fusion.3
  191.4 0.7 copy_dynamic-update-slice_fusion
  192.2 6.1 %fusion.13 = bf16[2,30,512]{2,1,0:T(8,128)(2,1)S(1)} fusion(bf16[27,512,256,1,1,1]{2,1,0,5,4,3:T(8,128)(2,1)} %bitcast.145, bf16[2,1,2,30,2,27,256]{6,3,5,4,2,0,1:T(8,128)(2,1)} %copy_dynamic-update-slice_fusion), kind=kOutput, calls=%fused_computation.29 | convolution fusion | flops 1698785280 | bytes 10457088 | tf_op jit(solution)/shard_map/dot_general | solution.py:54
  198.3 0.7 copy.192
  199.0 40.6 %all-reduce.7.cloned.1.call-done = f32[8,3,3,3,256]{4,0,1,3,2:T(8,128)} async-done(((f32[8,3,3,3,256]{4,0,1,3,2:T(8,128)}), f32[8,3,3,3,256]{4,0,1,3,2:T(8,128)}) %all-reduce.7.cloned.1.call-update) | async-done | bytes 221200
  239.6 1.0 constant_dynamic-slice_fusion
  (57 shorter events, 10.9 us)
Async XLA Ops:
  7.2 29.9 %copy-start.1 = (bf16[1,2,2,60,256]{4,2,3,1,0:T(2,128)(2,1)S(1)}, bf16[1,2,2,60,256]{4,2,3,1,0:T(2,128)(2,1)}, u32[]{:S(2)}) copy-start(bf16[1,2,2,60,256]{4,2,3,1,0:T(2,128)(2,1)} %param.4) | copy-start | bytes 368644
  7.2 5.7 %collective-permute-start.1 = (bf16[1,2,1,30,512]{4,1,3,2,0:T(2,128)(2,1)}, bf16[1,2,1,30,512]{4,1,3,2,0:T(2,128)(2,1)S(1)}, u32[]{:S(2)}, u32[]{:S(2)}) collective-permute-start(bf16[1,2,1,30,512]{4,1,3,2,0:T(2,128)(2,1)} %param.3), channel_id=1, source_target_pairs={{0,16},{16,32},{32,48},{1,17},{17,33},{33,49},{2,18},{18,34},{34,5... | collective-permute-start | bytes 184328 | tf_op jit(solution)/shard_map/ppermute | solution.py:10
  15.0 28.2 %copy-start.2 = (u32[256]{0:T(256)S(1)}, u32[256]{0:T(256)}, u32[]{:S(2)}) copy-start(u32[256]{0:T(256)} %constant.32) | copy-start | bytes 3076
  39.4 51.1 %all-to-all-start = ((bf16[16,2,2,60,256]{4,2,3,1,0:T(2,128)(2,1)}), bf16[16,2,2,60,256]{4,2,3,1,0:T(2,128)(2,1)S(1)}, u32[]{:S(2)}, u32[]{:S(2)}) async-start(bf16[16,2,2,60,256]{4,2,3,1,0:T(2,128)(2,1)} %stack.129), calls=%async_computation | async-start | bytes 3932160 | tf_op jit(solution)/shard_map/all_to_all | solution.py:38
  43.1 149.0 %reduce-scatter.3.cloned.1.call-start = ((), (), s32[]{:S(2)}) async-start(), calls=%async_computation.3 | async-start | bytes 1105920 | tf_op jit(solution)/shard_map/reduce_scatter | solution.py:79
  90.5 1.3 copy-start
  155.6 14.3 %collective-permute-start = (bf16[2,4,60,256]{3,2,1,0:T(8,128)(2,1)S(1)}, bf16[2,4,60,256]{3,2,1,0:T(8,128)(2,1)S(1)}, u32[]{:S(2)}, u32[]{:S(2)}) collective-permute-start(bf16[2,4,60,256]{3,2,1,0:T(8,128)(2,1)S(1)} %pad_dynamic-slice_fusion.3), channel_id=1, source_target_pairs={{16,0},{32,16},{48,32},{17,1},{33,17},{49,33},{18,2},{34,18},{50,3... | collective-permute-start | bytes 737288 | tf_op jit(solution)/shard_map/ppermute | solution.py:10
  169.7 69.8 %all-reduce.7.cloned.1.call-start = ((), (), s32[]{:S(2)}) async-start(), calls=%async_computation.4 | async-start | bytes 442368
Sparse Core Ops, SparseCore 0:
  169.9 18.0 reduce-scatter.2
  192.3 47.2 all-reduce.6
